TPU v7x, 32 devices: a whole 2x2x4 slice. The times are simulated.
32 devices in a mesh: dp: 8 (over z, x), seq: 4 (over y, core).
Axes of the slice: x: 2, y: 2, z: 4, core: 2. Of those that a mesh axis runs over, the one named last changes fastest.
Arguments:
- queries: bfloat16 [8, 512, 32, 128], P('dp', 'seq'), may hold values from -13 to 13
- keys: bfloat16 [8, 512, 4, 128], P('dp', 'seq'), may hold values from -13 to 13
- values: bfloat16 [8, 512, 4, 128], P('dp', 'seq'), may hold values from -6 to 6
- d_out: bfloat16 [8, 512, 32, 128], P('dp', 'seq'), may hold values from -6 to 6
- doc_ids: int32 [8, 512], P('dp', 'seq'), may hold values from 0 to 3, never falling along the last dimension, each value on 1 to 256 neighbouring positions
Outputs:
- query_grad: bfloat16 [8, 512, 32, 128], P('dp', 'seq')
- key_grad: bfloat16 [8, 512, 4, 128], P('dp', 'seq')
- value_grad: bfloat16 [8, 512, 4, 128], P('dp', 'seq')
- value_bias_grad: float32 [512], P('dp')
Inputs may be any that keep to these rules, and one draw needn't show every extreme that they name: `doc_ids`: in each row the ids never fall along the tokens; each of the 4 ids marks one document of 1 to 256 tokens, and one document has exactly 256.
All inputs are finite; a program needn't handle non-finite values.
Results may differ from a plain program's by a relative error of at most 0.0073.
Values may be sent and summed in bfloat16 or wider, within the bound.
No kernel may reach another device: no remote copies, remote signals or barrier semaphores. Data moves between devices by JAX's collectives and lax.ppermute only.
A program may use at most 64 MiB of HBM per device.

v0:
```python
import math
import jax
import jax.numpy as jnp
from jax import lax
from jax.sharding import PartitionSpec as P

masked_score = -1e30


def tile_terms(
    query_block,
    grad_block,
    block_of_keys,
    block_of_values,
    query_docs,
    key_docs,
    query_first,
    key_first,
    score_scale,
):
    scores = (
        jnp.einsum("qhd,kd->hqk", query_block, block_of_keys, preferred_element_type=jnp.float32)
        * score_scale
    )
    dweights = jnp.einsum(
        "qhd,kd->hqk", grad_block, block_of_values, preferred_element_type=jnp.float32
    )
    rows_per_block = query_block.shape[0]
    query_place = query_first + jnp.arange(rows_per_block)
    key_place = key_first + jnp.arange(rows_per_block)
    allowed = (key_place[None, :] <= query_place[:, None]) & (
        key_docs[None, :] == query_docs[:, None]
    )
    masked = jnp.where(allowed[None], scores, masked_score)
    return (masked, dweights, allowed)


def shards(queries, keys, values, d_out, doc_ids):
    seq_size = lax.axis_size("seq")
    query_local = queries[0]
    grad_local = d_out[0]
    key_local = keys[0]
    value_local = values[0]
    kv_heads = key_local.shape[1]
    head_dim = key_local.shape[2]
    local_tokens = query_local.shape[0]
    head_copies = seq_size // kv_heads
    documents_per_row = lax.all_gather(doc_ids[0], "seq", axis=0, tiled=True)
    query_row, grad_row = (
        lax.all_to_all(query_local, "seq", split_axis=1, concat_axis=0, tiled=True),
        lax.all_to_all(grad_local, "seq", split_axis=1, concat_axis=0, tiled=True),
    )
    key_copies, value_copies = (
        lax.all_to_all(
            jnp.repeat(key_local, head_copies, axis=1),
            "seq",
            split_axis=1,
            concat_axis=0,
            tiled=True,
        ),
        lax.all_to_all(
            jnp.repeat(value_local, head_copies, axis=1),
            "seq",
            split_axis=1,
            concat_axis=0,
            tiled=True,
        ),
    )
    row_of_keys = key_copies[:, 0]
    row_of_values = value_copies[:, 0]
    row_length = query_row.shape[0]
    local_heads = query_row.shape[1]
    rows_per_block = min(512, row_length)
    block_count = row_length // rows_per_block
    score_scale = 1.0 / math.sqrt(head_dim)
    doc_blocks = documents_per_row.reshape(block_count, rows_per_block)
    lowest = jnp.sum((doc_blocks[None, :, -1] < doc_blocks[:, None, 0]).astype(jnp.int32), axis=1)

    def select_block(array, index):
        return lax.dynamic_slice_in_dim(array, index * rows_per_block, rows_per_block, 0)

    def row_stats(qindex):
        query_block = select_block(query_row, qindex)
        grad_block = select_block(grad_row, qindex)
        query_docs = select_block(documents_per_row, qindex)

        def row_tile_step(key_index, running_total):
            row_top, exp_total, weighted = running_total
            masked, dweights, allowed = tile_terms(
                query_block,
                grad_block,
                select_block(row_of_keys, key_index),
                select_block(row_of_values, key_index),
                query_docs,
                select_block(documents_per_row, key_index),
                qindex * rows_per_block,
                key_index * rows_per_block,
                score_scale,
            )
            new_top = jnp.maximum(row_top, jnp.max(masked, axis=2))
            factor = jnp.exp(row_top - new_top)
            exponent = jnp.where(allowed[None], jnp.exp(masked - new_top[:, :, None]), 0.0)
            return (
                new_top,
                exp_total * factor + jnp.sum(exponent, axis=2),
                weighted * factor + jnp.sum(exponent * dweights, axis=2),
            )

        zeros = jnp.zeros((local_heads, rows_per_block), jnp.float32)
        first_state = (
            jnp.full((local_heads, rows_per_block), masked_score, jnp.float32),
            zeros,
            zeros,
        )
        row_top, exp_total, weighted = lax.fori_loop(
            lowest[qindex], qindex + 1, row_tile_step, first_state
        )
        return (row_top, exp_total, weighted / exp_total)

    row_tops, row_totals, row_deltas = lax.map(row_stats, jnp.arange(block_count))

    def backward(qindex, running_total):
        query_all, key_acc, value_acc = running_total
        query_block = select_block(query_row, qindex)
        grad_block = select_block(grad_row, qindex)
        query_docs = select_block(documents_per_row, qindex)
        row_top = row_tops[qindex]
        exp_total = row_totals[qindex]
        row_delta = row_deltas[qindex]

        def backward_tile_step(key_index, inner_product):
            query_acc, key_inner_product, value_inner_product = inner_product
            block_of_keys = select_block(row_of_keys, key_index)
            block_of_values = select_block(row_of_values, key_index)
            masked, dweights, allowed = tile_terms(
                query_block,
                grad_block,
                block_of_keys,
                block_of_values,
                query_docs,
                select_block(documents_per_row, key_index),
                qindex * rows_per_block,
                key_index * rows_per_block,
                score_scale,
            )
            weights = jnp.where(
                allowed[None], jnp.exp(masked - row_top[:, :, None]) / exp_total[:, :, None], 0.0
            )
            dscores = weights * (dweights - row_delta[:, :, None])
            weights_half = weights.astype(jnp.bfloat16)
            dscores_half = dscores.astype(jnp.bfloat16)
            query_acc = query_acc + jnp.einsum(
                "hqk,kd->qhd", dscores_half, block_of_keys, preferred_element_type=jnp.float32
            )
            key_piece = jnp.einsum(
                "hqk,qhd->kd", dscores_half, query_block, preferred_element_type=jnp.float32
            )
            value_piece = jnp.einsum(
                "hqk,qhd->kd", weights_half, grad_block, preferred_element_type=jnp.float32
            )
            key_inner_product = lax.dynamic_update_slice_in_dim(
                key_inner_product,
                select_block(key_inner_product, key_index) + key_piece,
                key_index * rows_per_block,
                0,
            )
            value_inner_product = lax.dynamic_update_slice_in_dim(
                value_inner_product,
                select_block(value_inner_product, key_index) + value_piece,
                key_index * rows_per_block,
                0,
            )
            return (query_acc, key_inner_product, value_inner_product)

        query_start = jnp.zeros((rows_per_block, local_heads, head_dim), jnp.float32)
        query_acc, key_acc, value_acc = lax.fori_loop(
            lowest[qindex], qindex + 1, backward_tile_step, (query_start, key_acc, value_acc)
        )
        query_all = lax.dynamic_update_slice_in_dim(
            query_all, query_acc, qindex * rows_per_block, 0
        )
        return (query_all, key_acc, value_acc)

    start_state = (
        jnp.zeros((row_length, local_heads, head_dim), jnp.float32),
        jnp.zeros((row_length, head_dim), jnp.float32),
        jnp.zeros((row_length, head_dim), jnp.float32),
    )
    query_all, key_acc, value_acc = lax.fori_loop(0, block_count, backward, start_state)
    query_half = (query_all * score_scale).astype(jnp.bfloat16)
    key_half = (key_acc * score_scale).astype(jnp.bfloat16)[:, None]
    value_half = value_acc.astype(jnp.bfloat16)[:, None]
    query_grad, key_back, value_back = (
        lax.all_to_all(query_half, "seq", split_axis=0, concat_axis=1, tiled=True),
        lax.all_to_all(key_half, "seq", split_axis=0, concat_axis=1, tiled=True),
        lax.all_to_all(value_half, "seq", split_axis=0, concat_axis=1, tiled=True),
    )
    summed_key = jnp.sum(
        key_back.reshape(local_tokens, kv_heads, head_copies, head_dim), axis=2, dtype=jnp.float32
    )
    summed_value = jnp.sum(
        value_back.reshape(local_tokens, kv_heads, head_copies, head_dim), axis=2, dtype=jnp.float32
    )
    partial_value = jnp.sum(summed_value, axis=0).reshape(-1)
    row_bias = lax.psum_scatter(partial_value, "dp", scatter_dimension=0, tiled=True)
    total_bias = lax.psum(row_bias, "seq")
    total_tokens = local_tokens * seq_size * lax.axis_size("dp")
    return (
        query_grad[None],
        summed_key.astype(jnp.bfloat16)[None],
        summed_value.astype(jnp.bfloat16)[None],
        total_bias / math.sqrt(total_tokens),
    )


def solution(mesh):
    placed = (
        P("dp", "seq", None, None),
        P("dp", "seq", None, None),
        P("dp", "seq", None, None),
        P("dp", "seq", None, None),
        P("dp", "seq"),
    )
    return jax.shard_map(
        shards,
        mesh=mesh,
        in_specs=placed,
        out_specs=(
            P("dp", "seq", None, None),
            P("dp", "seq", None, None),
            P("dp", "seq", None, None),
            P("dp"),
        ),
        check_vma=False,
    )
```

profile of v0, /device:TPU:0, one launch (start us, length us, event | category | flops | bytes accessed | tf_op | source)
XLA Modules:
  0.0 128.4 jit_solution(110084953796103875)
XLA Ops:
  0.7 1.6 %copy.62 = bf16[1,128,4,128]{3,1,2,0:T(8,128)(2,1)} copy(bf16[1,128,4,128]{3,2,1,0:T(4,128)(2,1)} %param.10) | data formatting | bytes 262144 | tf_op args[1]
  2.3 4.3 %all-to-all-start = ((bf16[128,4,128]{2,0,1:T(8,128)(2,1)}), bf16[128,4,128]{2,0,1:T(8,128)(2,1)S(1)}, u32[]{:S(2)}, u32[]{:S(2)}) async-start(bf16[128,4,128]{2,0,1:T(8,128)(2,1)} %bitcast.125), calls=%async_computation | async-start | bytes 262144 | tf_op jit(solution)/shard_map/all_to_all | solution.py:54
  6.5 2.6 %copy.60 = bf16[1,128,32,128]{3,1,2,0:T(8,128)(2,1)} copy(bf16[1,128,32,128]{3,2,1,0:T(8,128)(2,1)} %param.9) | data formatting | bytes 2097152 | tf_op args[0]
  9.1 2.0 %all-to-all-done = bf16[128,4,128]{2,0,1:T(8,128)(2,1)S(1)} async-done(((bf16[128,4,128]{2,0,1:T(8,128)(2,1)}), bf16[128,4,128]{2,0,1:T(8,128)(2,1)S(1)}, u32[]{:S(2)}, u32[]{:S(2)}) %all-to-all-start) | async-done | bytes 131104 | tf_op jit(solution)/shard_map/all_to_all | solution.py:54
  11.1 3.5 %all-to-all-start.1 = ((bf16[128,32,128]{2,0,1:T(8,128)(2,1)}), bf16[128,32,128]{2,0,1:T(8,128)(2,1)S(1)}, u32[]{:S(2)}, u32[]{:S(2)}) async-start(bf16[128,32,128]{2,0,1:T(8,128)(2,1)} %bitcast.123), calls=%async_computation.1 | async-start | bytes 2097152 | tf_op jit(solution)/shard_map/all_to_all | solution.py:50
  14.7 2.6 %copy.59 = bf16[1,128,32,128]{3,1,2,0:T(8,128)(2,1)} copy(bf16[1,128,32,128]{3,2,1,0:T(8,128)(2,1)} %param.12) | data formatting | bytes 2097152 | tf_op args[3]
  17.3 11.8 %all-to-all-done.1 = bf16[128,32,128]{2,0,1:T(8,128)(2,1)S(1)} async-done(((bf16[128,32,128]{2,0,1:T(8,128)(2,1)}), bf16[128,32,128]{2,0,1:T(8,128)(2,1)S(1)}, u32[]{:S(2)}, u32[]{:S(2)}) %all-to-all-start.1) | async-done | bytes 1048608 | tf_op jit(solution)/shard_map/all_to_all | solution.py:50
  29.1 3.5 %all-to-all-start.3 = ((bf16[128,32,128]{2,0,1:T(8,128)(2,1)}), bf16[128,32,128]{2,0,1:T(8,128)(2,1)S(1)}, u32[]{:S(2)}, u32[]{:S(2)}) async-start(bf16[128,32,128]{2,0,1:T(8,128)(2,1)} %bitcast.122), calls=%async_computation.3 | async-start | bytes 2097152 | tf_op jit(solution)/shard_map/all_to_all | solution.py:51
  33.3 14.6 %all-gather = s32[1,512]{1,0:T(1,128)S(1)} all-gather(s32[1,128]{1,0:T(1,128)S(1)} %copy-done.3), channel_id=2, replica_groups=mesh['dp'=8,'seq'=4] {'seq'}, dimensions={1}, use_global_device_ids=true | all-gather | bytes 2560 | tf_op jit(solution)/shard_map/all_gather | solution.py:48
  47.9 3.3 %all-to-all-start.2 = ((bf16[128,4,128]{2,0,1:T(8,128)(2,1)}), bf16[128,4,128]{2,0,1:T(8,128)(2,1)S(1)}, u32[]{:S(2)}, u32[]{:S(2)}) async-start(bf16[128,4,128]{2,0,1:T(8,128)(2,1)} %bitcast.124), calls=%async_computation.2 | async-start | bytes 262144 | tf_op jit(solution)/shard_map/all_to_all | solution.py:61
  53.3 2.5 %all-to-all-done.2 = bf16[128,4,128]{2,0,1:T(8,128)(2,1)S(1)} async-done(((bf16[128,4,128]{2,0,1:T(8,128)(2,1)}), bf16[128,4,128]{2,0,1:T(8,128)(2,1)S(1)}, u32[]{:S(2)}, u32[]{:S(2)}) %all-to-all-start.2) | async-done | bytes 131104 | tf_op jit(solution)/shard_map/all_to_all | solution.py:61
  55.8 6.9 %while.59 = (s32[]{:T(128)}, f32[8,512]{1,0:T(8,128)S(1)}, f32[8,512]{1,0:T(8,128)S(1)}, f32[8,512]{1,0:T(8,128)S(1)}, s32[512]{0:T(512)S(1)}, /*index=5*/bf16[5...) while((s32[]{:T(128)}, f32[8,512]{1,0:T(8,128)S(1)}, ...), condition=%wide.region_4.0_spmd, body=%wide.region_0.4_spmd.sunk | while | flops 1103901184 | bytes 28874876 | solution.py:115
  57.7 2.0 %fusion.65 = f32[8,512]{1,0:T(8,128)S(1)} fusion(f32[512,512,8]{1,0,2:T(8,128)S(1)} %get-tuple-element.705, f32[8,512]{1,0:T(8,128)S(1)} %max.9, pred[512,512]{0,1:T(8,128)(4,1)S(1)} %fusion.62), kind=kLoop, calls=%fused_computation.5.clone.1 | loop fusion | flops 10481664 | bytes 8683520 | tf_op jit(solution)/shard_map/while/body/eval_jaxpr/while/body/reduce_sum | solution.py:105
  59.7 3.0 %fusion.64 = f32[8,512]{1,0:T(8,128)S(1)} fusion(f32[512,512,8]{1,0,2:T(8,128)S(1)} %get-tuple-element.705, f32[8,512]{1,0:T(8,128)S(1)} %max.9, pred[512,512]{0,1:T(8,128)(4,1)S(1)} %fusion.62, bf16[512,8,128]{2,0,1:T(8,128)(2,1)S(1)} %get-tuple-element.750, bf16[512,128]{1,0:T(8,128)(2,1)S(1)} %get-tuple-element.749), kind=kOutput, calls=%fused_computation.1.clone.1 | convolution fusion | flops 549449728 | bytes 9863168 | tf_op jit(solution)/shard_map/while/body/eval_jaxpr/while/body/qhd,kd->hqk/dot_general | solution.py:25
  64.3 10.2 %while.60 = (s32[]{:T(128)}, f32[512,8,128]{2,0,1:T(8,128)}, f32[512,128]{1,0:T(8,128)S(1)}, f32[512,128]{1,0:T(8,128)S(1)}, s32[512]{0:T(512)S(1)}, /*index=5*/...) while((s32[]{:T(128)}, f32[512,8,128]{2,0,1:T(8,128)}, ...), condition=%wide.region_6.7_spmd, body=%wide.region_5.0_spmd.sunk | while | flops 2704671232 | bytes 64936140 | solution.py:176
  64.6 2.9 %fusion.77 = f32[8,512,512]{1,2,0:T(8,128)S(1)} fusion(f32[8,512]{1,0:T(8,128)S(1)} %bitcast.190, f32[8,512]{1,0:T(8,128)S(1)} %bitcast.184, pred[512,512]{0,1:T(8,128)(4,1)S(1)} %fusion.76, bf16[512,8,128]{2,0,1:T(8,128)(2,1)S(1)} %get-tuple-element.787, bf16[512,128]{1,0:T(8,128)(2,1)S(1)} %get-tuple-element.786), kind=kOutput, calls=%fused_computation.22.clone.1 | convolution fusion | flops 547356672 | bytes 9863168 | tf_op jit(solution)/shard_map/while/body/eval_jaxpr/while/body/qhd,kd->hqk/dot_general | solution.py:22
  71.5 1.7 %bitcast_add_fusion.2 = f32[512,8,128]{2,0,1:T(8,128)S(1)} fusion(f32[512,8,128]{2,0,1:T(8,128)S(1)} %copy-done, bf16[8,512,512]{1,2,0:T(8,128)(2,1)S(1)} %fusion.78, bf16[512,128]{1,0:T(8,128)(2,1)S(1)} %get-tuple-element.786), kind=kOutput, calls=%fused_computation.25.clone.1 | convolution fusion | flops 537395200 | bytes 8519680 | tf_op jit(solution)/shard_map/while/body/eval_jaxpr/while/body/hqk,kd->qhd/dot_general | solution.py:152
  76.4 3.3 %all-to-all-start.5 = ((bf16[4,2,8192]{2,1,0:T(2,128)(2,1)}), bf16[4,2,8192]{2,1,0:T(2,128)(2,1)S(1)}, u32[]{:S(2)}, u32[]{:S(2)}) async-start(bf16[4,2,8192]{2,1,0:T(2,128)(2,1)} %reshape.211), calls=%async_computation.5 | async-start | bytes 262144 | tf_op jit(solution)/shard_map/all_to_all | solution.py:195
  81.1 3.2 %all-to-all-done.5 = bf16[4,2,8192]{2,1,0:T(2,128)(2,1)S(1)} async-done(((bf16[4,2,8192]{2,1,0:T(2,128)(2,1)}), bf16[4,2,8192]{2,1,0:T(2,128)(2,1)S(1)}, u32[]{:S(2)}, u32[]{:S(2)}) %all-to-all-start.5) | async-done | bytes 131104 | tf_op jit(solution)/shard_map/all_to_all | solution.py:195
  84.3 3.3 %all-to-all-start.6 = ((bf16[4,2,8192]{2,1,0:T(2,128)(2,1)}), bf16[4,2,8192]{2,1,0:T(2,128)(2,1)S(1)}, u32[]{:S(2)}, u32[]{:S(2)}) async-start(bf16[4,2,8192]{2,1,0:T(2,128)(2,1)} %reshape.213), calls=%async_computation.6 | async-start | bytes 262144 | tf_op jit(solution)/shard_map/all_to_all | solution.py:196
  87.7 3.9 %fusion.26 = bf16[512,8,128]{2,1,0:T(8,128)(2,1)} fusion(f32[512,8,128]{2,0,1:T(8,128)} %get-tuple-element.519), kind=kLoop, calls=%fused_computation.37 | loop fusion | flops 1048576 | bytes 3145728 | tf_op jit(solution)/shard_map/convert_element_type | solution.py:190
  92.2 3.5 %all-to-all-start.4 = ((bf16[512,8,128]{2,1,0:T(8,128)(2,1)}), bf16[512,8,128]{2,1,0:T(8,128)(2,1)S(1)}, u32[]{:S(2)}, u32[]{:S(2)}) async-start(bf16[512,8,128]{2,1,0:T(8,128)(2,1)} %fusion.26), calls=%async_computation.4 | async-start | bytes 2097152 | tf_op jit(solution)/shard_map/all_to_all | solution.py:194
  98.9 22.1 %all-reduce = f32[512]{0:T(512)S(1)} all-reduce(f32[512]{0:T(512)S(1)} %bitcast.193), channel_id=3, replica_groups=mesh['dp'=8,'seq'=4] {'dp'}, use_global_device_ids=true, to_apply=%region_8.9.clone | all-reduce | flops 512 | bytes 4096
  121.1 5.6 %psum.7 = f32[64]{0:T(128)S(1)} all-reduce(f32[64]{0:T(128)S(1)} %dynamic-slice.4), channel_id=1, replica_groups=mesh['dp'=8,'seq'=4] {'seq'}, use_global_device_ids=true, to_apply=%region_9.10 | all-reduce | flops 64 | bytes 512 | tf_op jit(solution)/shard_map/psum | solution.py:206
  (52 shorter events, 18.5 us)
Async XLA Ops:
  0.6 31.9 %copy-start.2 = (bf16[1,128,4,128]{3,2,1,0:T(4,128)(2,1)S(1)}, bf16[1,128,4,128]{3,2,1,0:T(4,128)(2,1)}, u32[]{:S(2)}) copy-start(bf16[1,128,4,128]{3,2,1,0:T(4,128)(2,1)} %param.11) | copy-start | bytes 393220
  0.6 32.6 %copy-start.3 = (s32[1,128]{1,0:T(1,128)S(1)}, s32[1,128]{1,0:T(1,128)}, u32[]{:S(2)}) copy-start(s32[1,128]{1,0:T(1,128)} %param.13) | copy-start | bytes 1540
  2.3 8.9 %all-to-all-start = ((bf16[128,4,128]{2,0,1:T(8,128)(2,1)}), bf16[128,4,128]{2,0,1:T(8,128)(2,1)S(1)}, u32[]{:S(2)}, u32[]{:S(2)}) async-start(bf16[128,4,128]{2,0,1:T(8,128)(2,1)} %bitcast.125), calls=%async_computation | async-start | bytes 262144 | tf_op jit(solution)/shard_map/all_to_all | solution.py:54
  11.1 17.9 %all-to-all-start.1 = ((bf16[128,32,128]{2,0,1:T(8,128)(2,1)}), bf16[128,32,128]{2,0,1:T(8,128)(2,1)S(1)}, u32[]{:S(2)}, u32[]{:S(2)}) async-start(bf16[128,32,128]{2,0,1:T(8,128)(2,1)} %bitcast.123), calls=%async_computation.1 | async-start | bytes 2097152 | tf_op jit(solution)/shard_map/all_to_all | solution.py:50
  29.1 18.8 %all-to-all-start.3 = ((bf16[128,32,128]{2,0,1:T(8,128)(2,1)}), bf16[128,32,128]{2,0,1:T(8,128)(2,1)S(1)}, u32[]{:S(2)}, u32[]{:S(2)}) async-start(bf16[128,32,128]{2,0,1:T(8,128)(2,1)} %bitcast.122), calls=%async_computation.3 | async-start | bytes 2097152 | tf_op jit(solution)/shard_map/all_to_all | solution.py:51
  47.9 7.9 %all-to-all-start.2 = ((bf16[128,4,128]{2,0,1:T(8,128)(2,1)}), bf16[128,4,128]{2,0,1:T(8,128)(2,1)S(1)}, u32[]{:S(2)}, u32[]{:S(2)}) async-start(bf16[128,4,128]{2,0,1:T(8,128)(2,1)} %bitcast.124), calls=%async_computation.2 | async-start | bytes 262144 | tf_op jit(solution)/shard_map/all_to_all | solution.py:61
  64.3 31.4 %copy-start.4 = (u32[32]{0:T(128)S(1)}, u32[32]{0:T(128)}, u32[]{:S(2)}) copy-start(u32[32]{0:T(128)} %constant.142) | copy-start | bytes 388
  68.9 2.6 %copy-start = (f32[512,8,128]{2,0,1:T(8,128)S(1)}, f32[512,8,128]{2,0,1:T(8,128)}, u32[]{:S(2)}) copy-start(f32[512,8,128]{2,0,1:T(8,128)} %get-tuple-element.768) | copy-start | bytes 6291460 | tf_op jit(solution)/shard_map/while/body/eval_jaxpr/while
  73.1 1.3 %copy-start.1 = (f32[512,8,128]{2,0,1:T(8,128)}, f32[512,8,128]{2,0,1:T(8,128)S(1)}, u32[]{:S(2)}) copy-start(f32[512,8,128]{2,0,1:T(8,128)S(1)} %bitcast_add_fusion.2) | copy-start | bytes 6291460 | tf_op jit(solution)/shard_map/while/body/eval_jaxpr/while
  76.4 7.9 %all-to-all-start.5 = ((bf16[4,2,8192]{2,1,0:T(2,128)(2,1)}), bf16[4,2,8192]{2,1,0:T(2,128)(2,1)S(1)}, u32[]{:S(2)}, u32[]{:S(2)}) async-start(bf16[4,2,8192]{2,1,0:T(2,128)(2,1)} %reshape.211), calls=%async_computation.5 | async-start | bytes 262144 | tf_op jit(solution)/shard_map/all_to_all | solution.py:195
  84.3 7.9 %all-to-all-start.6 = ((bf16[4,2,8192]{2,1,0:T(2,128)(2,1)}), bf16[4,2,8192]{2,1,0:T(2,128)(2,1)S(1)}, u32[]{:S(2)}, u32[]{:S(2)}) async-start(bf16[4,2,8192]{2,1,0:T(2,128)(2,1)} %reshape.213), calls=%async_computation.6 | async-start | bytes 262144 | tf_op jit(solution)/shard_map/all_to_all | solution.py:196
  92.2 35.0 %all-to-all-start.4 = ((bf16[512,8,128]{2,1,0:T(8,128)(2,1)}), bf16[512,8,128]{2,1,0:T(8,128)(2,1)S(1)}, u32[]{:S(2)}, u32[]{:S(2)}) async-start(bf16[512,8,128]{2,1,0:T(8,128)(2,1)} %fusion.26), calls=%async_computation.4 | async-start | bytes 2097152 | tf_op jit(solution)/shard_map/all_to_all | solution.py:194
where the time goes:
time: 129 us; the launch traced here: 128 us
  blocking collectives  42.4 us (33%)
  starting transfers between devices  24.8 us (19%)
  waiting for transfers between devices  20.1 us (16%)
  local copies, waits for them, and re-layouts  16.7 us (13%)
  matrix products  13 us (10%)
  other arithmetic  8.5 us (7%)
  between operations  2.77 us (2%)
    unnamed x1, blocking collectives  22.1 us
    all_gather x1, blocking collectives, shards(): documents_per_row = lax.all_gather(doc_ids[0], 'seq', axis=0, tiled=True)  14.6 us
    all_to_all x1, waiting for transfers between devices, shards(): lax.all_to_all(query_local, 'seq', split_axis=1, concat_axis=0, tiled=True)  11.8 us
    unnamed x20, local copies, waits for them, and re-layouts  11.4 us
    psum x1, blocking collectives, shards(): total_bias = lax.psum(row_bias, 'seq')  5.63 us
    dot_general x2, matrix products, tile_terms(): jnp.einsum('qhd,kd->hqk', query_block, block_of_keys, preferred_element_t...  4.44 us
    dot_general x2, matrix products, tile_terms(): jnp.einsum('qhd,kd->hqk', grad_block, block_of_values, preferred_element_...  4.28 us
    all_to_all x1, starting transfers between devices, shards(): lax.all_to_all(jnp.repeat(key_local, head_copies, axis=1), 'seq', split_a...  4.26 us
  transfers between devices with their start and end apart: 7, of which 5 were waited for; matrix products, arithmetic and copies ran while one was open for 12% of the time, Pallas kernels for 0%

commit v1 on v0

--- a/solution.py
+++ b/solution.py
@@ -5,6 +5,13 @@
 from jax.sharding import PartitionSpec as P
 
 masked_score = -1e30
+
+
+def swap_blocks(x, name, split, join):
+    size = lax.axis_size(name)
+    blocks = jnp.stack(jnp.split(x, size, axis=split), axis=0)
+    blocks = lax.all_to_all(blocks, name, split_axis=0, concat_axis=0)
+    return jnp.concatenate(blocks, axis=join)
 
 
 def tile_terms(
@@ -47,7 +54,7 @@
     head_copies = seq_size // kv_heads
     documents_per_row = lax.all_gather(doc_ids[0], "seq", axis=0, tiled=True)
     query_row, grad_row = (
-        lax.all_to_all(query_local, "seq", split_axis=1, concat_axis=0, tiled=True),
+        swap_blocks(query_local, "seq", 1, 0),
         lax.all_to_all(grad_local, "seq", split_axis=1, concat_axis=0, tiled=True),
     )
     key_copies, value_copies = (

time: 129 us -> 129 us (level)
    all_to_all x1, waiting for transfers between devices: 0.01 us -> 12 us  [shards(): lax.all_to_all(grad_local, 'seq', split_axis=1, concat_axis=0, tiled=True)]
    all_to_all x1, waiting for transfers between devices: 11.8 us -> 0.01 us  [swap_blocks(): blocks = lax.all_to_all(blocks, name, split_axis=0, concat_axis=0)]
    unnamed x20 -> x19, local copies, waits for them, and re-layouts: 11.4 us -> 8.75 us
    another operation x6 -> x7, local copies, waits for them, and re-layouts: 1.56 us -> 2.84 us
where the time goes in v1:
time: 129 us; the launch traced here: 128 us
  blocking collectives  42.4 us (33%)
  starting transfers between devices  24.8 us (19%)
  waiting for transfers between devices  20.2 us (16%)
  local copies, waits for them, and re-layouts  15.5 us (12%)
  matrix products  13 us (10%)
  other arithmetic  9.6 us (7%)
  between operations  2.78 us (2%)
    unnamed x1, blocking collectives  22.1 us
    all_gather x1, blocking collectives, shards(): documents_per_row = lax.all_gather(doc_ids[0], 'seq', axis=0, tiled=True)  14.6 us
    all_to_all x1, waiting for transfers between devices, shards(): lax.all_to_all(grad_local, 'seq', split_axis=1, concat_axis=0, tiled=True)  12 us
    unnamed x19, local copies, waits for them, and re-layouts  8.75 us
    psum x1, blocking collectives, shards(): total_bias = lax.psum(row_bias, 'seq')  5.63 us
    dot_general x2, matrix products, tile_terms(): jnp.einsum('qhd,kd->hqk', query_block, block_of_keys, preferred_element_t...  4.44 us
    dot_general x2, matrix products, tile_terms(): jnp.einsum('qhd,kd->hqk', grad_block, block_of_values, preferred_element_...  4.28 us
    all_to_all x1, starting transfers between devices, shards(): lax.all_to_all(jnp.repeat(key_local, head_copies, axis=1), 'seq', split_a...  4.26 us
  transfers between devices with their start and end apart: 7, of which 5 were waited for; matrix products, arithmetic and copies ran while one was open for 12% of the time, Pallas kernels for 0%

profile of v1, /device:TPU:0, one launch (start us, length us, event | category | flops | bytes accessed | tf_op | source)
XLA Modules:
  0.0 128.4 jit_solution(1781094178856411546)
XLA Ops:
  0.7 1.6 %copy.58 = bf16[1,128,4,128]{3,1,2,0:T(8,128)(2,1)} copy(bf16[1,128,4,128]{3,2,1,0:T(4,128)(2,1)} %param.10) | data formatting | bytes 262144 | tf_op args[1]
  2.3 4.3 %all-to-all-start = ((bf16[128,4,128]{2,0,1:T(8,128)(2,1)}), bf16[128,4,128]{2,0,1:T(8,128)(2,1)S(1)}, u32[]{:S(2)}, u32[]{:S(2)}) async-start(bf16[128,4,128]{2,0,1:T(8,128)(2,1)} %bitcast.128), calls=%async_computation | async-start | bytes 262144 | tf_op jit(solution)/shard_map/all_to_all | solution.py:61
  6.5 2.6 %copy.56 = bf16[1,128,32,128]{3,1,2,0:T(8,128)(2,1)} copy(bf16[1,128,32,128]{3,2,1,0:T(8,128)(2,1)} %param.12) | data formatting | bytes 2097152 | tf_op args[3]
  9.1 2.0 %all-to-all-done = bf16[128,4,128]{2,0,1:T(8,128)(2,1)S(1)} async-done(((bf16[128,4,128]{2,0,1:T(8,128)(2,1)}), bf16[128,4,128]{2,0,1:T(8,128)(2,1)S(1)}, u32[]{:S(2)}, u32[]{:S(2)}) %all-to-all-start) | async-done | bytes 131104 | tf_op jit(solution)/shard_map/all_to_all | solution.py:61
  11.1 3.5 %all-to-all-start.3 = ((bf16[128,32,128]{2,0,1:T(8,128)(2,1)}), bf16[128,32,128]{2,0,1:T(8,128)(2,1)S(1)}, u32[]{:S(2)}, u32[]{:S(2)}) async-start(bf16[128,32,128]{2,0,1:T(8,128)(2,1)} %bitcast.126), calls=%async_computation.3 | async-start | bytes 2097152 | tf_op jit(solution)/shard_map/all_to_all | solution.py:58
  17.1 12.0 %all-to-all-done.3 = bf16[128,32,128]{2,0,1:T(8,128)(2,1)S(1)} async-done(((bf16[128,32,128]{2,0,1:T(8,128)(2,1)}), bf16[128,32,128]{2,0,1:T(8,128)(2,1)S(1)}, u32[]{:S(2)}, u32[]{:S(2)}) %all-to-all-start.3) | async-done | bytes 1048608 | tf_op jit(solution)/shard_map/all_to_all | solution.py:58
  29.1 3.5 %all-to-all-start.1 = ((bf16[4,128,8,128]{3,2,1,0:T(8,128)(2,1)}), bf16[4,128,8,128]{3,2,1,0:T(8,128)(2,1)S(1)}, u32[]{:S(2)}, u32[]{:S(2)}) async-start(bf16[4,128,8,128]{3,2,1,0:T(8,128)(2,1)} %pad_maximum_fusion), calls=%async_computation.1 | async-start | bytes 2097152 | tf_op jit(solution)/shard_map/all_to_all | solution.py:13
  33.3 14.6 %all-gather = s32[1,512]{1,0:T(1,128)S(1)} all-gather(s32[1,128]{1,0:T(1,128)S(1)} %copy-done.3), channel_id=2, replica_groups=mesh['dp'=8,'seq'=4] {'seq'}, dimensions={1}, use_global_device_ids=true | all-gather | bytes 2560 | tf_op jit(solution)/shard_map/all_gather | solution.py:55
  47.9 3.3 %all-to-all-start.2 = ((bf16[128,4,128]{2,0,1:T(8,128)(2,1)}), bf16[128,4,128]{2,0,1:T(8,128)(2,1)S(1)}, u32[]{:S(2)}, u32[]{:S(2)}) async-start(bf16[128,4,128]{2,0,1:T(8,128)(2,1)} %bitcast.127), calls=%async_computation.2 | async-start | bytes 262144 | tf_op jit(solution)/shard_map/all_to_all | solution.py:68
  53.5 2.3 %all-to-all-done.2 = bf16[128,4,128]{2,0,1:T(8,128)(2,1)S(1)} async-done(((bf16[128,4,128]{2,0,1:T(8,128)(2,1)}), bf16[128,4,128]{2,0,1:T(8,128)(2,1)S(1)}, u32[]{:S(2)}, u32[]{:S(2)}) %all-to-all-start.2) | async-done | bytes 131104 | tf_op jit(solution)/shard_map/all_to_all | solution.py:68
  55.8 6.9 %while.59 = (s32[]{:T(128)}, f32[8,512]{1,0:T(8,128)S(1)}, f32[8,512]{1,0:T(8,128)S(1)}, f32[8,512]{1,0:T(8,128)S(1)}, s32[512]{0:T(512)S(1)}, /*index=5*/bf16[5...) while((s32[]{:T(128)}, f32[8,512]{1,0:T(8,128)S(1)}, ...), condition=%wide.region_4.0_spmd, body=%wide.region_0.4_spmd.sunk | while | flops 1103901184 | bytes 28874876 | solution.py:122
  56.1 1.5 %fusion.63 = (f32[8,512]{1,0:T(8,128)S(1)}, f32[512,512,8]{1,0,2:T(8,128)S(1)}) fusion(pred[512,512]{0,1:T(8,128)(4,1)S(1)} %fusion.62, bf16[512,8,128]{2,0,1:T(8,128)(2,1)S(1)} %get-tuple-element.752, bf16[512,128]{1,0:T(8,128)(2,1)S(1)} %get-tuple-element.751), kind=kOutput, calls=%fused_computation.4.clone.1 | convolution fusion | flops 543158272 | bytes 9846784 | tf_op jit(solution)/shard_map/while/body/eval_jaxpr/while/body/qhd,kd->hqk/dot_general | solution.py:29
  57.7 2.0 %fusion.65 = f32[8,512]{1,0:T(8,128)S(1)} fusion(f32[512,512,8]{1,0,2:T(8,128)S(1)} %get-tuple-element.709, f32[8,512]{1,0:T(8,128)S(1)} %max.9, pred[512,512]{0,1:T(8,128)(4,1)S(1)} %fusion.62), kind=kLoop, calls=%fused_computation.5.clone.1 | loop fusion | flops 10481664 | bytes 8683520 | tf_op jit(solution)/shard_map/while/body/eval_jaxpr/while/body/reduce_sum | solution.py:112
  59.7 3.0 %fusion.64 = f32[8,512]{1,0:T(8,128)S(1)} fusion(f32[512,512,8]{1,0,2:T(8,128)S(1)} %get-tuple-element.709, f32[8,512]{1,0:T(8,128)S(1)} %max.9, pred[512,512]{0,1:T(8,128)(4,1)S(1)} %fusion.62, bf16[512,8,128]{2,0,1:T(8,128)(2,1)S(1)} %get-tuple-element.754, bf16[512,128]{1,0:T(8,128)(2,1)S(1)} %get-tuple-element.753), kind=kOutput, calls=%fused_computation.1.clone.1 | convolution fusion | flops 549449728 | bytes 9863168 | tf_op jit(solution)/shard_map/while/body/eval_jaxpr/while/body/qhd,kd->hqk/dot_general | solution.py:32
  64.3 10.2 %while.60 = (s32[]{:T(128)}, f32[512,8,128]{2,0,1:T(8,128)}, f32[512,128]{1,0:T(8,128)S(1)}, f32[512,128]{1,0:T(8,128)S(1)}, s32[512]{0:T(512)S(1)}, /*index=5*/...) while((s32[]{:T(128)}, f32[512,8,128]{2,0,1:T(8,128)}, ...), condition=%wide.region_6.7_spmd, body=%wide.region_5.0_spmd.sunk | while | flops 2704671232 | bytes 64936140 | solution.py:183
  64.6 2.9 %fusion.77 = f32[8,512,512]{1,2,0:T(8,128)S(1)} fusion(f32[8,512]{1,0:T(8,128)S(1)} %bitcast.193, f32[8,512]{1,0:T(8,128)S(1)} %bitcast.186, pred[512,512]{0,1:T(8,128)(4,1)S(1)} %fusion.76, bf16[512,8,128]{2,0,1:T(8,128)(2,1)S(1)} %get-tuple-element.791, bf16[512,128]{1,0:T(8,128)(2,1)S(1)} %get-tuple-element.790), kind=kOutput, calls=%fused_computation.22.clone.1 | convolution fusion | flops 547356672 | bytes 9863168 | tf_op jit(solution)/shard_map/while/body/eval_jaxpr/while/body/qhd,kd->hqk/dot_general | solution.py:29
  71.5 1.7 %bitcast_add_fusion.2 = f32[512,8,128]{2,0,1:T(8,128)S(1)} fusion(f32[512,8,128]{2,0,1:T(8,128)S(1)} %copy-done, bf16[8,512,512]{1,2,0:T(8,128)(2,1)S(1)} %fusion.78, bf16[512,128]{1,0:T(8,128)(2,1)S(1)} %get-tuple-element.790), kind=kOutput, calls=%fused_computation.25.clone.1 | convolution fusion | flops 537395200 | bytes 8519680 | tf_op jit(solution)/shard_map/while/body/eval_jaxpr/while/body/hqk,kd->qhd/dot_general | solution.py:159
  76.4 3.3 %all-to-all-start.5 = ((bf16[4,2,8192]{2,1,0:T(2,128)(2,1)}), bf16[4,2,8192]{2,1,0:T(2,128)(2,1)S(1)}, u32[]{:S(2)}, u32[]{:S(2)}) async-start(bf16[4,2,8192]{2,1,0:T(2,128)(2,1)} %reshape.215), calls=%async_computation.5 | async-start | bytes 262144 | tf_op jit(solution)/shard_map/all_to_all | solution.py:202
  81.1 3.2 %all-to-all-done.5 = bf16[4,2,8192]{2,1,0:T(2,128)(2,1)S(1)} async-done(((bf16[4,2,8192]{2,1,0:T(2,128)(2,1)}), bf16[4,2,8192]{2,1,0:T(2,128)(2,1)S(1)}, u32[]{:S(2)}, u32[]{:S(2)}) %all-to-all-start.5) | async-done | bytes 131104 | tf_op jit(solution)/shard_map/all_to_all | solution.py:202
  84.3 3.3 %all-to-all-start.6 = ((bf16[4,2,8192]{2,1,0:T(2,128)(2,1)}), bf16[4,2,8192]{2,1,0:T(2,128)(2,1)S(1)}, u32[]{:S(2)}, u32[]{:S(2)}) async-start(bf16[4,2,8192]{2,1,0:T(2,128)(2,1)} %reshape.217), calls=%async_computation.6 | async-start | bytes 262144 | tf_op jit(solution)/shard_map/all_to_all | solution.py:203
  87.6 3.9 %fusion.26 = bf16[512,8,128]{2,1,0:T(8,128)(2,1)} fusion(f32[512,8,128]{2,0,1:T(8,128)} %get-tuple-element.519), kind=kLoop, calls=%fused_computation.37 | loop fusion | flops 1048576 | bytes 3145728 | tf_op jit(solution)/shard_map/convert_element_type | solution.py:197
  92.2 3.5 %all-to-all-start.4 = ((bf16[512,8,128]{2,1,0:T(8,128)(2,1)}), bf16[512,8,128]{2,1,0:T(8,128)(2,1)S(1)}, u32[]{:S(2)}, u32[]{:S(2)}) async-start(bf16[512,8,128]{2,1,0:T(8,128)(2,1)} %fusion.26), calls=%async_computation.4 | async-start | bytes 2097152 | tf_op jit(solution)/shard_map/all_to_all | solution.py:201
  98.9 22.1 %all-reduce = f32[512]{0:T(512)S(1)} all-reduce(f32[512]{0:T(512)S(1)} %bitcast.196), channel_id=3, replica_groups=mesh['dp'=8,'seq'=4] {'dp'}, use_global_device_ids=true, to_apply=%region_8.9.clone | all-reduce | flops 512 | bytes 4096
  121.1 5.6 %psum.7 = f32[64]{0:T(128)S(1)} all-reduce(f32[64]{0:T(128)S(1)} %dynamic-slice.4), channel_id=1, replica_groups=mesh['dp'=8,'seq'=4] {'seq'}, use_global_device_ids=true, to_apply=%region_9.10 | all-reduce | flops 64 | bytes 512 | tf_op jit(solution)/shard_map/psum | solution.py:213
  (53 shorter events, 19.5 us)
Async XLA Ops:
  0.6 31.9 %copy-start.2 = (bf16[1,128,4,128]{3,2,1,0:T(4,128)(2,1)S(1)}, bf16[1,128,4,128]{3,2,1,0:T(4,128)(2,1)}, u32[]{:S(2)}) copy-start(bf16[1,128,4,128]{3,2,1,0:T(4,128)(2,1)} %param.11) | copy-start | bytes 393220
  0.6 32.6 %copy-start.3 = (s32[1,128]{1,0:T(1,128)S(1)}, s32[1,128]{1,0:T(1,128)}, u32[]{:S(2)}) copy-start(s32[1,128]{1,0:T(1,128)} %param.13) | copy-start | bytes 1540
  2.3 8.9 %all-to-all-start = ((bf16[128,4,128]{2,0,1:T(8,128)(2,1)}), bf16[128,4,128]{2,0,1:T(8,128)(2,1)S(1)}, u32[]{:S(2)}, u32[]{:S(2)}) async-start(bf16[128,4,128]{2,0,1:T(8,128)(2,1)} %bitcast.128), calls=%async_computation | async-start | bytes 262144 | tf_op jit(solution)/shard_map/all_to_all | solution.py:61
  11.1 17.9 %all-to-all-start.3 = ((bf16[128,32,128]{2,0,1:T(8,128)(2,1)}), bf16[128,32,128]{2,0,1:T(8,128)(2,1)S(1)}, u32[]{:S(2)}, u32[]{:S(2)}) async-start(bf16[128,32,128]{2,0,1:T(8,128)(2,1)} %bitcast.126), calls=%async_computation.3 | async-start | bytes 2097152 | tf_op jit(solution)/shard_map/all_to_all | solution.py:58
  29.1 18.8 %all-to-all-start.1 = ((bf16[4,128,8,128]{3,2,1,0:T(8,128)(2,1)}), bf16[4,128,8,128]{3,2,1,0:T(8,128)(2,1)S(1)}, u32[]{:S(2)}, u32[]{:S(2)}) async-start(bf16[4,128,8,128]{3,2,1,0:T(8,128)(2,1)} %pad_maximum_fusion), calls=%async_computation.1 | async-start | bytes 2097152 | tf_op jit(solution)/shard_map/all_to_all | solution.py:13
  47.9 7.9 %all-to-all-start.2 = ((bf16[128,4,128]{2,0,1:T(8,128)(2,1)}), bf16[128,4,128]{2,0,1:T(8,128)(2,1)S(1)}, u32[]{:S(2)}, u32[]{:S(2)}) async-start(bf16[128,4,128]{2,0,1:T(8,128)(2,1)} %bitcast.127), calls=%async_computation.2 | async-start | bytes 262144 | tf_op jit(solution)/shard_map/all_to_all | solution.py:68
  64.3 31.4 %copy-start.4 = (u32[32]{0:T(128)S(1)}, u32[32]{0:T(128)}, u32[]{:S(2)}) copy-start(u32[32]{0:T(128)} %constant.142) | copy-start | bytes 388
  68.8 2.6 %copy-start = (f32[512,8,128]{2,0,1:T(8,128)S(1)}, f32[512,8,128]{2,0,1:T(8,128)}, u32[]{:S(2)}) copy-start(f32[512,8,128]{2,0,1:T(8,128)} %get-tuple-element.772) | copy-start | bytes 6291460 | tf_op jit(solution)/shard_map/while/body/eval_jaxpr/while
  73.1 1.3 %copy-start.1 = (f32[512,8,128]{2,0,1:T(8,128)}, f32[512,8,128]{2,0,1:T(8,128)S(1)}, u32[]{:S(2)}) copy-start(f32[512,8,128]{2,0,1:T(8,128)S(1)} %bitcast_add_fusion.2) | copy-start | bytes 6291460 | tf_op jit(solution)/shard_map/while/body/eval_jaxpr/while
  76.4 7.9 %all-to-all-start.5 = ((bf16[4,2,8192]{2,1,0:T(2,128)(2,1)}), bf16[4,2,8192]{2,1,0:T(2,128)(2,1)S(1)}, u32[]{:S(2)}, u32[]{:S(2)}) async-start(bf16[4,2,8192]{2,1,0:T(2,128)(2,1)} %reshape.215), calls=%async_computation.5 | async-start | bytes 262144 | tf_op jit(solution)/shard_map/all_to_all | solution.py:202
  84.3 7.9 %all-to-all-start.6 = ((bf16[4,2,8192]{2,1,0:T(2,128)(2,1)}), bf16[4,2,8192]{2,1,0:T(2,128)(2,1)S(1)}, u32[]{:S(2)}, u32[]{:S(2)}) async-start(bf16[4,2,8192]{2,1,0:T(2,128)(2,1)} %reshape.217), calls=%async_computation.6 | async-start | bytes 262144 | tf_op jit(solution)/shard_map/all_to_all | solution.py:203
  92.2 35.0 %all-to-all-start.4 = ((bf16[512,8,128]{2,1,0:T(8,128)(2,1)}), bf16[512,8,128]{2,1,0:T(8,128)(2,1)S(1)}, u32[]{:S(2)}, u32[]{:S(2)}) async-start(bf16[512,8,128]{2,1,0:T(8,128)(2,1)} %fusion.26), calls=%async_computation.4 | async-start | bytes 2097152 | tf_op jit(solution)/shard_map/all_to_all | solution.py:201
